TPU v7x, 32 devices: a whole 2x2x4 slice. The times are simulated.
32 devices in a mesh: ty: 4 (over y, x), tx: 8 (over z, core).
Axes of the slice: x: 2, y: 2, z: 4, core: 2. Of those that a mesh axis runs over, the one named last changes fastest.
Arguments:
- block_sums: float32 [4096, 1, 1024], P(('ty', 'tx')), may hold values from -6 to 6
- block_weights: float32 [4096, 1, 1024], P(('ty', 'tx')), may hold values from 0.1 to 2
- block_tile: int32 [4096, 1], P(('ty', 'tx')), may hold values from 0 to 31; in each aligned block of 128 rows (0 to 127, 128 to 255, ...) at most 8 rows name the same one
- block_row: int32 [4096], P(('ty', 'tx')), may hold values from 0 to 127
- prior_weight: float32 [512, 8192], P('ty', 'tx'), may hold values from 0.1 to 1
Outputs:
- solution_field: float32 [512, 8192], P('ty', 'tx')
- residual: float32 [512, 8192], P('ty', 'tx')
Inputs may be any that keep to these rules, and one draw needn't show every extreme that they name: `block_tile`: among the 128 blocks of one log shard no tile is named more than 8 times, a bound that some block reaches.
All inputs are finite; a program needn't handle non-finite values.
Results may differ from a plain program's by a relative error of at most 0.0003.
Values sent between devices are 32-bit elements; how exact they have to be, the bound alone decides.
A program may use at most 64 MiB of HBM per device.

v0:
```python
import functools

import jax
import jax.numpy as jnp
import numpy as np
from jax import lax
from jax.experimental import pallas as pl
from jax.experimental.pallas import tpu as pltpu
from jax.sharding import PartitionSpec as P

HALF = 32
LANES = 128
PIECES = 5
LIMIT = 20 * 1024 * 1024
MESH = pl.DeviceIdType.MESH


def taps_matrix(offset):
    def weight(distance):
        scaled = np.abs(distance) / (HALF + 1.0)
        value = (1.0 - scaled) ** 4 * (1.0 + 4.0 * scaled)
        return np.where(np.abs(distance) <= HALF, value, 0.0)

    total = np.sum(weight(np.arange(-HALF, HALF + 1).astype(np.float64)))
    return (weight(offset.astype(np.float64)) / total).astype(np.float32)


def halves(values):
    high = values.astype(jnp.bfloat16)
    return high, (values - high.astype(jnp.float32)).astype(jnp.bfloat16)


def kernel_matrices(rows, width):
    row = np.arange(rows)[:, None] - (np.arange(rows + 2 * HALF)[None, :] - HALF)
    col = (np.arange(width + 2 * LANES)[:, None] - LANES) - np.arange(width)[None, :]
    row_high, row_low = halves(jnp.asarray(taps_matrix(row)))
    col_high, col_low = halves(jnp.asarray(taps_matrix(col)))
    return jnp.concatenate([row_high, row_low], axis=0), col_high, col_low


def directions():
    return [(dy, dx) for dy in (-1, 0, 1) for dx in (-1, 0, 1) if (dy, dx) != (0, 0)]


def span(step, size, margin, width, sending):
    if step == 0:
        return pl.ds(margin, size)
    if sending:
        return pl.ds(margin, width) if step < 0 else pl.ds(margin + size - width, width)
    return pl.ds(margin + size, width) if step < 0 else pl.ds(margin - width, width)


def dot(left, right):
    return jnp.dot(left, right, preferred_element_type=jnp.float32)


def cross(left, right):
    return lax.dot_general(
        left, right, (((0,), (0,)), ((), ())), preferred_element_type=jnp.float32
    )


def iota(shape, dim):
    return lax.broadcasted_iota(jnp.int32, shape, dim)


def ones(mask):
    return jnp.where(mask, 1.0, 0.0).astype(jnp.bfloat16)


def total(values):
    return jnp.sum(values, axis=(0, 1), keepdims=True)


def solve_kernel(
    ny,
    nx,
    slots,
    direct,
    room,
    tile_hbm,
    band_hbm,
    sums_hbm,
    weights_hbm,
    prior_hbm,
    row_hbm,
    col_high_hbm,
    col_low_hbm,
    r0_ref,
    u_ref,
    z_ref,
    scalars_ref,
    tile_ref,
    band_ref,
    sums_ref,
    weights_ref,
    prior_ref,
    row_ref,
    col_high_ref,
    col_low_ref,
    root_ref,
    load_sem,
    send_table,
    got_table,
    send_near,
    got_near,
    send_far,
    got_far,
    send_spill,
    got_spill,
    send_relay,
    got_relay,
    send_list,
    got_list,
    pad_a,
    pad_b,
    part,
    parts,
    table_sem,
    near_sem,
    far_sem,
    spill_sem,
    relay_sem,
    halo_send,
    halo_recv,
    part_sem,
):
    count = ny * nx
    side_x = nx // 2
    flat_x = side_x // 2
    peers = ny * side_x
    spill = slots - direct
    blocks, groups, _ = sums_ref.shape
    rows, cols = prior_ref.shape
    width = col_high_ref.shape[1]
    ty, tx = lax.axis_index("ty"), lax.axis_index("tx")
    me = ty * nx + tx
    side = tx // side_x
    inner_x = lax.rem(tx, side_x)
    here = ty * side_x + inner_x
    far_side = 1 - side

    def device(index):
        hop = index // ny
        sign = 1 - 2 * lax.rem(hop, 2)
        other_x = lax.rem(tx + nx // 2 + nx + sign * ((hop + 1) // 2), nx)
        return lax.rem(ty + ny // 2 + index, ny), other_x

    barrier = pltpu.get_barrier_semaphore()

    def greet(index, carry):
        other_y, other_x = device(index)

        @pl.when(other_y * nx + other_x != me)
        def _():
            pl.semaphore_signal(
                barrier, inc=1, device_id=(other_y, other_x), device_id_type=MESH
            )

        return carry

    loads = [
        pltpu.make_async_copy(source, target, load_sem.at[index])
        for index, (source, target) in enumerate(
            (
                (tile_hbm, tile_ref),
                (band_hbm, band_ref),
                (sums_hbm, sums_ref),
                (weights_hbm, weights_ref),
                (row_hbm, row_ref),
                (col_high_hbm, col_high_ref),
                (col_low_hbm, col_low_ref),
                (prior_hbm, prior_ref),
            )
        )
    ]
    for load in loads[:4]:
        load.start()
    for pad in (pad_a, pad_b):
        pad[0:HALF, :] = jnp.zeros((HALF, cols + 2 * LANES), jnp.float32)
        pad[HALF + rows :, :] = jnp.zeros((HALF, cols + 2 * LANES), jnp.float32)
        pad[HALF : HALF + rows, 0:LANES] = jnp.zeros((rows, LANES), jnp.float32)
        pad[HALF : HALF + rows, LANES + cols :] = jnp.zeros((rows, LANES), jnp.float32)
    lax.fori_loop(0, count, greet, 0)
    for load in loads[4:]:
        load.start()

    loads[0].wait()
    loads[1].wait()
    tile = tile_ref[...]
    square = (blocks, blocks)
    down, across = iota(square, 0), iota(square, 1)

    def as_column(row):
        spread = jnp.broadcast_to(row, square)
        return jnp.sum(jnp.where(down == across, spread, 0), axis=1, keepdims=True)

    def before(column):
        return jnp.sum(jnp.where(down < across, column, 0), axis=0, keepdims=True)

    def before_column(row):
        return jnp.sum(jnp.where(across < down, row, 0), axis=1, keepdims=True)

    def seat(tiles):
        return tiles // nx * side_x + lax.rem(tiles, side_x)

    def crosses(tiles):
        return lax.rem(tiles, nx) // side_x != side

    tile_column = as_column(tile)
    same = jnp.where(tile_column == tile, 1, 0)
    rank, rank_column = before(same), before_column(same)
    near_rows, far_rows = peers * slots, peers * direct
    index = jnp.where(
        crosses(tile),
        near_rows + seat(tile) * direct + rank,
        seat(tile) * slots + rank,
    )
    if spill:
        over = jnp.where(crosses(tile) & (rank >= direct), 1, 0)
        over_column = jnp.where(crosses(tile_column) & (rank_column >= direct), 1, 0)
        turn = before(over_column)
        index = jnp.where(over > 0, jnp.where(turn < room, near_rows + far_rows + turn, -1), index)
        turn_column = before_column(over)
        listing = jnp.where(
            (turn_column == iota((blocks, LANES), 1)) & (over_column > 0),
            seat(tile_column) * spill + rank_column - direct + 1,
            0,
        )
        send_list[...] = jnp.sum(listing, axis=0, keepdims=True).astype(jnp.float32)
        excess = jnp.sum(over, axis=1, keepdims=True).astype(jnp.float32)
    place = ones(iota((near_rows + far_rows + room, blocks), 0) == index)
    place = jnp.concatenate([place, place], axis=1)
    owner = ones(iota((count, blocks), 0) == tile)
    numbers = jnp.where(
        rank_column == iota((blocks, LANES), 1), as_column(band_ref[...]) + 1, 0
    ).astype(jnp.float32)
    table = dot(owner, numbers.astype(jnp.bfloat16))
    if spill:
        table = jnp.where(iota((count, LANES), 1) == LANES - 1, excess, table)
    send_table[...] = table.reshape(count, 1, LANES)

    def pack(source, array):
        for group in range(0, groups, 2):
            window = slice(group * LANES, (group + 2) * LANES)
            values = jnp.concatenate([source[:, group, :], source[:, group + 1, :]], axis=1)
            moved = dot(place, jnp.concatenate(halves(values), axis=0))
            send_near[array, :, :, window] = moved[:near_rows].reshape(peers, slots, 2 * LANES)
            moved = moved[near_rows:]
            send_far[array, :, :, window] = moved[:far_rows].reshape(peers, direct, 2 * LANES)
            if spill:
                send_spill[array, :, window] = moved[far_rows:]

    def push(source, target, semaphores, which, other_y, other_x):
        pltpu.make_async_remote_copy(
            src_ref=source,
            dst_ref=target,
            send_sem=semaphores.at[0, which],
            recv_sem=semaphores.at[1, which],
            device_id=(other_y, other_x),
            device_id_type=MESH,
        ).start()

    def cut(ref, place, window):
        return ref.at[place] if window is None else ref.at[place, :, window]

    def route(source, target, semaphores, which, reach, window=None):
        def send(index, carry):
            other_y = lax.rem(ty + ny // 2 + index, ny)
            hop = index // ny
            if reach == "far":
                inner = lax.rem(inner_x + side_x // 2 + hop, side_x)
                other_x = inner + side_x * far_side
            else:
                layer = inner_x // flat_x
                layer = layer if reach == "flat" else 1 - layer
                inner = layer * flat_x + lax.rem(inner_x + flat_x // 2 + hop, flat_x)
                other_x = inner + side_x * side
            there = other_y * side_x + inner

            def go():
                push(
                    cut(source, there, window),
                    cut(target, here, window),
                    semaphores,
                    which,
                    other_y,
                    other_x,
                )

            if reach == "flat":
                pl.when(there != here)(go)
            else:
                go()
            return carry

        lax.fori_loop(0, peers if reach == "far" else ny * flat_x, send, 0)

    def share(source_of, target, semaphores):
        def send(index, carry):
            other_y, other_x = device(index)
            other = other_y * nx + other_x

            @pl.when(other != me)
            def _():
                push(source_of(other), target.at[me], semaphores, 0, other_y, other_x)

            return carry

        lax.fori_loop(0, count, send, 0)

    def mirror(source, target, semaphores, which):
        push(source, target, semaphores, which, ty, inner_x + side_x * far_side)

    def drain(ref, semaphores, way, which):
        pltpu.make_async_copy(ref, ref, semaphores.at[way, which]).wait()

    def arrived(target, semaphores, which, number, window=None, way=1):
        drain(cut(target, pl.ds(0, number), window), semaphores, way, which)

    def exchange(pad, phase, start, size):
        copies = []
        for index, (dy, dx) in enumerate(directions()):
            if (dx < 0 and start > 0) or (dx > 0 and start + size < cols):
                continue
            middle = pl.ds(LANES + start, size)
            copy = pltpu.make_async_remote_copy(
                src_ref=pad.at[
                    span(dy, rows, HALF, HALF, True),
                    span(dx, cols, LANES, LANES, True) if dx else middle,
                ],
                dst_ref=pad.at[
                    span(dy, rows, HALF, HALF, False),
                    span(dx, cols, LANES, LANES, False) if dx else middle,
                ],
                send_sem=halo_send.at[phase, index],
                recv_sem=halo_recv.at[phase, index],
                device_id=(
                    lax.rem(ty + dy + ny, ny),
                    lax.rem(tx + dx + nx, nx),
                ),
                device_id_type=MESH,
            )
            goes = (ty + dy >= 0) & (ty + dy < ny) & (tx + dx >= 0) & (tx + dx < nx)
            comes = (ty - dy >= 0) & (ty - dy < ny) & (tx - dx >= 0) & (tx - dx < nx)
            copies.append((copy, goes, comes))
            pl.when(goes)(copy.start)
        return copies

    def receive(copies):
        for copy, goes, comes in copies:
            pl.when(comes)(copy.wait_recv)

    def finish(copies):
        for copy, goes, comes in copies:
            pl.when(goes)(copy.wait_send)

    def smooth(pad):
        high, low = halves(pad[...])
        both = dot(row_ref[...], high)
        down = both[:rows] + both[rows:] + dot(row_ref[0:rows, :], low)
        high, low = halves(down)
        stacked = jnp.concatenate([high, low], axis=0)
        pieces = []
        for left in range(0, cols, width):
            window = slice(left, left + width + 2 * LANES)
            both = dot(stacked[:, window], col_high_ref[...])
            pieces.append(both[:rows] + both[rows:] + dot(high[:, window], col_low_ref[...]))
        return jnp.concatenate(pieces, axis=1)

    quarter, eighth = cols // 4, cols // 8
    cuts = [(0, quarter), (3 * quarter, quarter), (quarter, quarter)]
    cuts += [(2 * quarter, eighth), (2 * quarter + eighth, eighth)]
    windows = [pl.ds(start, size) for start, size in cuts]

    def supply(piece):
        route(send_far.at[1], got_far.at[1], far_sem, 1 + piece, "far", windows[piece])

    def supply_near(array, reach, which, window=None):
        route(send_near.at[array], got_near.at[array], near_sem, which, reach, window)

    def settle_flat(ref, array, semaphores, which, way=1):
        arrived(ref.at[array], semaphores, which, ny * flat_x - 1, way=way)

    def settle_rise(ref, array, semaphores, which, window=None, way=1):
        arrived(ref.at[array], semaphores, which, ny * flat_x, window, way=way)

    loads[2].wait()
    pack(sums_ref, 0)
    loads[3].wait()
    pack(weights_ref, 1)
    pl.semaphore_wait(barrier, count - 1)
    if spill:
        mirror(send_list, got_list, spill_sem, 2)
        mirror(send_spill.at[0], got_spill.at[0], spill_sem, 0)
    share(lambda other: send_table.at[other], got_table, table_sem)
    supply_near(0, "rise", 1)
    route(send_far.at[0], got_far.at[0], far_sem, 0, "far")
    supply_near(0, "flat", 0)
    supply_near(1, "flat", 2)
    got_table[pl.ds(me, 1)] = send_table[pl.ds(me, 1)]
    for array in range(2):
        got_near[array, pl.ds(here, 1)] = send_near[array, pl.ds(here, 1)]

    def supply_relay(array, reach, which, window=None):
        route(send_relay.at[array], got_relay.at[array], relay_sem, which, reach, window)

    def relay(array):
        drain(got_spill.at[array], spill_sem, 1, array)
        moved = dot(hand, jnp.concatenate(halves(got_spill[array]), axis=0))
        send_relay[array] = moved.reshape(peers, spill, cols)
        got_relay[array, pl.ds(here, 1)] = send_relay[array, pl.ds(here, 1)]

    if spill:
        drain(got_list, spill_sem, 1, 2)
        named = got_list[...][:, :room]
        hand = ones(iota((peers * spill, room), 0).astype(jnp.float32) + 1.0 == named)
        hand = jnp.concatenate([hand, hand], axis=1)
        relay(0)
        supply_relay(0, "rise", 1)
        supply_relay(0, "flat", 0)
        mirror(send_spill.at[1], got_spill.at[1], spill_sem, 1)

    arrived(got_table, table_sem, 0, count - 1)
    slot = iota((1, count * slots), 1)
    past = slot - near_rows
    line = jnp.where(past < 0, slot // slots, past // direct)
    rank = jnp.where(past < 0, lax.rem(slot, slots), lax.rem(past, direct))
    if spill:
        later = past - far_rows
        line = jnp.where(later < 0, line, later // spill)
        rank = jnp.where(later < 0, rank, direct + lax.rem(later, spill))
    origin = line // side_x * nx + lax.rem(line, side_x)
    origin = origin + side_x * jnp.where(past < 0, side, far_side)
    table = got_table[...].reshape(count, LANES)
    listed = cross(table.astype(jnp.bfloat16), ones(iota((count, count * slots), 0) == origin))
    listed = jnp.where(iota(listed.shape, 0) == rank, listed, 0.0)
    listed = jnp.sum(listed, axis=0, keepdims=True)
    select = ones(iota((rows, count * slots), 0).astype(jnp.float32) + 1.0 == listed)

    def gather(array, window):
        def lines(ref, number):
            values = ref[array, :, :, window]
            return values.reshape(peers * number, values.shape[-1])

        values = [lines(got_near, slots), lines(got_far, direct)]
        if spill:
            values.append(lines(got_relay, spill))
        high, low = halves(jnp.concatenate(values, axis=0))
        return dot(select, high) + dot(select, low)

    settle_flat(got_near, 0, near_sem, 0)
    settle_rise(got_near, 0, near_sem, 1)
    arrived(got_far.at[0], far_sem, 0, peers)
    if spill:
        settle_flat(got_relay, 0, relay_sem, 0)
        settle_rise(got_relay, 0, relay_sem, 1)
    pad_a[HALF : HALF + rows, LANES : LANES + cols] = gather(0, slice(None))
    first = exchange(pad_a, 0, 0, cols)
    supply(0)
    supply_near(1, "rise", 3, windows[0])
    if spill:
        relay(1)
        supply_relay(1, "flat", 2)
    for piece, window in enumerate(windows):
        if piece > 0:
            supply_near(1, "rise", 3 + piece, window)
        if spill:
            supply_relay(1, "rise", 3 + piece, window)
        if piece > 0:
            supply(piece)
    for load in loads[4:]:
        load.wait()
    receive(first)
    u_ref[...] = smooth(pad_a)

    second = []
    settle_flat(got_near, 1, near_sem, 2)
    if spill:
        settle_flat(got_relay, 1, relay_sem, 2)
    for piece, window in enumerate(windows):
        left, size = cuts[piece]
        inner = slice(LANES + left, LANES + left + size)
        settle_rise(got_near, 1, near_sem, 3 + piece, window)
        if spill:
            settle_rise(got_relay, 1, relay_sem, 3 + piece, window)
        arrived(got_far.at[1], far_sem, 1 + piece, peers, window)
        root = jnp.sqrt(prior_ref[:, window] + gather(1, window))
        root_ref[:, window] = root
        r0_ref[:, window] = pad_a[HALF : HALF + rows, inner] / root
        u = root * u_ref[:, window]
        u_ref[:, window] = u
        pad_b[HALF : HALF + rows, inner] = root * u
        second += exchange(pad_b, 1 + piece, left, size)
    r0, u = r0_ref[...], u_ref[...]
    rr, ru = total(r0 * r0), total(r0 * u)
    own = jnp.where(rr > 0.0, ru / rr, 0.0)
    receive(second)
    z = root_ref[...] * smooth(pad_b)
    z_ref[...] = z
    q = own * r0 - u
    g = own * u - z
    lane = iota((1, LANES), 1)
    packed = jnp.zeros((1, LANES), jnp.float32)
    for index, value in enumerate((rr, ru, total(q * q), total(q * g), total(r0 * g))):
        packed = jnp.where(lane == index, value, packed)
    part[...] = packed
    parts[pl.ds(me, 1), 0, :] = packed
    share(lambda other: part, parts, part_sem)
    arrived(parts, part_sem, 0, count - 1)

    table = parts[...].reshape(count, LANES)
    rr_d, ru_d, qq_d, qg_d, rg_d = [table[:, i : i + 1] for i in range(5)]
    rr, ru = total(rr_d), total(ru_d)
    mu = ru / rr
    shift = mu - jnp.where(rr_d > 0.0, ru_d / rr_d, 0.0)
    qq = total(qq_d + shift * shift * rr_d)
    qg = total(qg_d + shift * (rg_d - qq_d) + shift * shift * ru_d)
    alpha0 = rr / (0.5 * rr + ru)
    norm = alpha0 * alpha0 * qq
    beta = norm / rr
    alpha1 = norm / (alpha0 * alpha0 * (0.5 * qq + qg) - beta * norm / alpha0)
    most = jnp.zeros((1, 1), jnp.float32)
    if spill:
        most = jnp.max(got_table[...].reshape(count, LANES), axis=0, keepdims=True)[:, LANES - 1 :]
    flag = jnp.where(most > room, 1.0, 0.0)
    packed = jnp.zeros((1, LANES), jnp.float32)
    for index, value in enumerate((alpha0, alpha1, beta, mu, flag)):
        packed = jnp.where(lane == index, value, packed)
    scalars_ref[...] = packed

    finish(first)
    finish(second)
    arrived(send_table, table_sem, 0, count - 1, way=0)
    for array in range(2):
        settle_flat(send_near, array, near_sem, 2 * array, way=0)
    settle_rise(send_near, 0, near_sem, 1, way=0)
    arrived(send_far.at[0], far_sem, 0, peers, way=0)
    for piece, window in enumerate(windows):
        arrived(send_far.at[1], far_sem, 1 + piece, peers, window, way=0)
        settle_rise(send_near, 1, near_sem, 3 + piece, window, way=0)
        if spill:
            settle_rise(send_relay, 1, relay_sem, 3 + piece, window, way=0)
    if spill:
        drain(send_list, spill_sem, 0, 2)
        for array in range(2):
            drain(send_spill.at[array], spill_sem, 0, array)
            settle_flat(send_relay, array, relay_sem, 2 * array, way=0)
        settle_rise(send_relay, 0, relay_sem, 1, way=0)
    arrived(parts, part_sem, 0, count - 1, way=0)


def close_kernel(r0_ref, u_ref, z_ref, scalars_ref, field_ref, residual_ref):
    alpha0, alpha1, beta, mu = [scalars_ref[0:1, i : i + 1] for i in range(4)]
    r0, u = r0_ref[...], u_ref[...]
    q = mu * r0 - u
    r1 = alpha0 * q
    field_ref[...] = alpha0 * r0 + alpha1 * (r1 + beta * r0)
    along = alpha0 * (0.5 * q + mu * u - z_ref[...]) + beta * (0.5 * r0 + u)
    residual_ref[...] = r1 - alpha1 * along


def solve(slots, direct, room, identity, arrays):
    ny, nx = lax.axis_size("ty"), lax.axis_size("tx")
    block_tile, block_row, block_sums, block_weights, prior_weight, *matrices = arrays
    count = ny * nx
    blocks, groups, _ = block_sums.shape
    rows, cols = prior_weight.shape
    peers = count // 2
    spill = max(slots - direct, 1)
    vmem = pl.BlockSpec(memory_space=pltpu.VMEM)
    hbm = pl.BlockSpec(memory_space=pltpu.HBM)
    shape = jax.ShapeDtypeStruct((rows, cols), jnp.float32)

    def scratch(*shape):
        return pltpu.VMEM(shape, jnp.float32)

    def semaphores(*shape):
        return pltpu.SemaphoreType.DMA(shape)

    def twice(*shape):
        return [scratch(*shape), scratch(*shape)]

    return pl.pallas_call(
        functools.partial(solve_kernel, ny, nx, slots, direct, room),
        out_shape=(shape, shape, shape, jax.ShapeDtypeStruct((1, LANES), jnp.float32)),
        in_specs=[hbm] * 8,
        out_specs=(vmem,) * 4,
        scratch_shapes=[
            pltpu.VMEM((1, blocks), jnp.int32),
            pltpu.VMEM((1, blocks), jnp.int32),
            *twice(blocks, groups, LANES),
            scratch(rows, cols),
            *[pltpu.VMEM(matrix.shape, matrix.dtype) for matrix in matrices],
            scratch(rows, cols),
            semaphores(8),
            *twice(count, 1, LANES),
            *twice(2, peers, slots, cols),
            *twice(2, peers, direct, cols),
            *twice(2, max(room, 8), cols),
            *twice(2, peers, spill, cols),
            *twice(1, LANES),
            *twice(rows + 2 * HALF, cols + 2 * LANES),
            scratch(1, LANES),
            scratch(count, 1, LANES),
            semaphores(2, 1),
            semaphores(2, 3 + PIECES),
            semaphores(2, 1 + PIECES),
            semaphores(2, 3),
            semaphores(2, 3 + PIECES),
            semaphores(1 + PIECES, 8),
            semaphores(1 + PIECES, 8),
            semaphores(2, 1),
        ],
        compiler_params=pltpu.CompilerParams(
            collective_id=identity, has_side_effects=True, vmem_limit_bytes=LIMIT
        ),
    )(*[pltpu.with_memory_space_constraint(array, pltpu.HBM) for array in arrays])


def close(r0, u, z, scalars):
    vmem = pl.BlockSpec(memory_space=pltpu.VMEM)
    shape = jax.ShapeDtypeStruct(r0.shape, jnp.float32)
    return pl.pallas_call(
        close_kernel, out_shape=(shape, shape), in_specs=[vmem] * 4, out_specs=(vmem, vmem),
        compiler_params=pltpu.CompilerParams(vmem_limit_bytes=LIMIT),
    )(r0, u, z, scalars)


def shards(block_sums, block_weights, block_tile, block_row, prior_weight):
    count = lax.axis_size("ty") * lax.axis_size("tx")
    blocks, band, cols = block_sums.shape
    slots = 2 * blocks // count
    arrays = (
        block_tile.reshape(1, blocks),
        block_row.reshape(1, blocks),
        block_sums.reshape(blocks * band, cols // LANES, LANES),
        block_weights.reshape(blocks * band, cols // LANES, LANES),
        prior_weight,
        *kernel_matrices(prior_weight.shape[0], 2 * LANES),
    )
    fields = solve(slots, slots // 2, blocks // 4, 0, arrays)
    return lax.cond(
        fields[3][0, 4] > 0.5,
        lambda fields: close(*solve(slots, slots, 0, 1, arrays)),
        lambda fields: close(*fields),
        fields,
    )


def solution(mesh):
    in_specs = (
        P(("ty", "tx"), None, None),
        P(("ty", "tx"), None, None),
        P(("ty", "tx"), None),
        P(("ty", "tx")),
        P("ty", "tx"),
    )
    out_specs = (P("ty", "tx"), P("ty", "tx"))
    return jax.shard_map(shards, mesh=mesh, in_specs=in_specs, out_specs=out_specs, check_vma=False)
```

profile of v0, /device:TPU:0, one launch (start us, length us, event | category | flops | bytes accessed | tf_op | source)
XLA Modules:
  0.0 63.8 jit_solution(5778190938082588546)
XLA Ops:
  0.6 60.4 %shard_map.90 = (f32[128,1024]{1,0:T(8,128)S(1)}, f32[128,1024]{1,0:T(8,128)S(1)}, f32[128,1024]{1,0:T(8,128)S(1)}, f32[1,128]{1,0:T(1,128)S(1)}) custom-call(s32[1,128]{1,0:T(1,128)} %bitcast.9, s32[1,128]{1,0:T(1,128)} %bitcast.11, f32[128,8,128]{2,1,0:T(8,128)} %bitcast.5, f32[128,8,128]{2,1,0:T(8,128)} %bitcast.7, f32[128,1024]{1,0:T(8,128)} %prior_hbm.1, ...), custom_call_target="tpu_custom_call" | custom-call | tf_op jit(solution)/shard_map/pallas_call | solution.py:584
  61.0 0.6 slice.3
  62.2 1.6 %conditional.1 = ((f32[128,1024]{1,0:T(8,128)}, f32[128,1024]{1,0:T(8,128)})) conditional(s32[]{:T(128)} %bitcast.4, (f32[128,1024]{1,0:T(8,128)S(1)}, f32[128,1024]{1,0:T(8,128)S(1)}, f32[128,1024]{1,0:T(8,128)S(1)}, f32[1,128]{1,0:T(1,128)S(1)}) %shard_map.90, (s32[1,128]{1,0:T(1,128)}, s32[1,128]{1,0:T(1,128)}, f32[128,8,128]{2,1,0:T(8,128)}, ...), branch_computations={%region_0.0_spmd, %region_1.0_spmd} | conditional | bytes 8 | solution.py:643
  62.2 1.6 %branch_0_fun.1 = (f32[128,1024]{1,0:T(8,128)}, f32[128,1024]{1,0:T(8,128)}) custom-call(f32[128,1024]{1,0:T(8,128)S(1)} %get-tuple-element.24.r0_ref, f32[128,1024]{1,0:T(8,128)S(1)} %get-tuple-element.25.u_ref, f32[128,1024]{1,0:T(8,128)S(1)} %get-tuple-element.26.z_ref, f32[1,128]{1,0:T(1,128)S(1)} %get-tuple-element.27.scalars_ref), custom_call_target="tpu_custom_call" | custom-call | tf_op jit(solution)/shard_map/cond/branch_0_fun/pallas_call | solution.py:624
where the time goes:
time: 64 us; the launch traced here: 63.8 us
  Pallas kernels  62 us (97%)
  between operations  1.29 us (2%)
    pallas_call x1, Pallas kernels, solve(): pl.pallas_call(functools.partial(solve_kernel, ny, nx, slots, direct, roo...  60.4 us
    pallas_call x1, Pallas kernels, close(): pl.pallas_call(close_kernel, out_shape=(shape, shape), in_specs=[vmem] *...  1.59 us

commit v1 on v0

--- a/solution.py
+++ b/solution.py
@@ -10,7 +10,9 @@
 
 HALF = 32
 LANES = 128
-PIECES = 5
+PIECES = 4
+EARLY = 2
+AHEAD = 1
 LIMIT = 20 * 1024 * 1024
 MESH = pl.DeviceIdType.MESH
 
@@ -174,6 +176,7 @@
             )
         )
     ]
+    lax.fori_loop(0, count, greet, 0, unroll=True)
     for load in loads[:4]:
         load.start()
     for pad in (pad_a, pad_b):
@@ -181,7 +184,6 @@
         pad[HALF + rows :, :] = jnp.zeros((HALF, cols + 2 * LANES), jnp.float32)
         pad[HALF : HALF + rows, 0:LANES] = jnp.zeros((rows, LANES), jnp.float32)
         pad[HALF : HALF + rows, LANES + cols :] = jnp.zeros((rows, LANES), jnp.float32)
-    lax.fori_loop(0, count, greet, 0)
     for load in loads[4:]:
         load.start()
 
@@ -294,7 +296,7 @@
                 go()
             return carry
 
-        lax.fori_loop(0, peers if reach == "far" else ny * flat_x, send, 0)
+        lax.fori_loop(0, peers if reach == "far" else ny * flat_x, send, 0, unroll=True)
 
     def share(source_of, target, semaphores):
         def send(index, carry):
@@ -307,7 +309,7 @@
 
             return carry
 
-        lax.fori_loop(0, count, send, 0)
+        lax.fori_loop(0, count, send, 0, unroll=True)
 
     def mirror(source, target, semaphores, which):
         push(source, target, semaphores, which, ty, inner_x + side_x * far_side)
@@ -369,21 +371,35 @@
         return jnp.concatenate(pieces, axis=1)
 
     quarter, eighth = cols // 4, cols // 8
-    cuts = [(0, quarter), (3 * quarter, quarter), (quarter, quarter)]
-    cuts += [(2 * quarter, eighth), (2 * quarter + eighth, eighth)]
+    cuts = [(0, quarter), (3 * quarter, quarter), (quarter, quarter), (2 * quarter, quarter)]
     windows = [pl.ds(start, size) for start, size in cuts]
 
-    def supply(piece):
-        route(send_far.at[1], got_far.at[1], far_sem, 1 + piece, "far", windows[piece])
-
-    def supply_near(array, reach, which, window=None):
-        route(send_near.at[array], got_near.at[array], near_sem, which, reach, window)
-
-    def settle_flat(ref, array, semaphores, which, way=1):
-        arrived(ref.at[array], semaphores, which, ny * flat_x - 1, way=way)
-
-    def settle_rise(ref, array, semaphores, which, window=None, way=1):
-        arrived(ref.at[array], semaphores, which, ny * flat_x, window, way=way)
+    def supply_far(array, piece):
+        which = array * PIECES + piece
+        route(send_far.at[array], got_far.at[array], far_sem, which, "far", windows[piece])
+
+    def supply_flat(source, target, semaphores, array):
+        route(source.at[array], target.at[array], semaphores, array, "flat")
+
+    def supply_rise(source, target, semaphores, array, piece):
+        which = 2 + array * PIECES + piece
+        route(source.at[array], target.at[array], semaphores, which, "rise", windows[piece])
+
+    def settle_flat(ref, semaphores, array, way=1):
+        arrived(ref.at[array], semaphores, array, ny * flat_x - 1, way=way)
+
+    def settle_rise(ref, semaphores, array, piece, way=1):
+        which = 2 + array * PIECES + piece
+        arrived(ref.at[array], semaphores, which, ny * flat_x, windows[piece], way=way)
+
+    def settle_far(ref, array, piece, way=1):
+        arrived(ref.at[array], far_sem, array * PIECES + piece, peers, windows[piece], way=way)
+
+    def settle_piece(array, piece):
+        settle_rise(got_near, near_sem, array, piece)
+        if spill:
+            settle_rise(got_relay, relay_sem, array, piece)
+        settle_far(got_far, array, piece)
 
     loads[2].wait()
     pack(sums_ref, 0)
@@ -394,16 +410,14 @@
         mirror(send_list, got_list, spill_sem, 2)
         mirror(send_spill.at[0], got_spill.at[0], spill_sem, 0)
     share(lambda other: send_table.at[other], got_table, table_sem)
-    supply_near(0, "rise", 1)
-    route(send_far.at[0], got_far.at[0], far_sem, 0, "far")
-    supply_near(0, "flat", 0)
-    supply_near(1, "flat", 2)
+    for piece in range(EARLY):
+        supply_rise(send_near, got_near, near_sem, 0, piece)
+        supply_far(0, piece)
+    for array in range(2):
+        supply_flat(send_near, got_near, near_sem, array)
     got_table[pl.ds(me, 1)] = send_table[pl.ds(me, 1)]
     for array in range(2):
         got_near[array, pl.ds(here, 1)] = send_near[array, pl.ds(here, 1)]
-
-    def supply_relay(array, reach, which, window=None):
-        route(send_relay.at[array], got_relay.at[array], relay_sem, which, reach, window)
 
     def relay(array):
         drain(got_spill.at[array], spill_sem, 1, array)
@@ -417,8 +431,15 @@
         hand = ones(iota((peers * spill, room), 0).astype(jnp.float32) + 1.0 == named)
         hand = jnp.concatenate([hand, hand], axis=1)
         relay(0)
-        supply_relay(0, "rise", 1)
-        supply_relay(0, "flat", 0)
+        for piece in range(EARLY):
+            supply_rise(send_relay, got_relay, relay_sem, 0, piece)
+    for piece in range(EARLY, PIECES):
+        supply_rise(send_near, got_near, near_sem, 0, piece)
+        if spill:
+            supply_rise(send_relay, got_relay, relay_sem, 0, piece)
+        supply_far(0, piece)
+    if spill:
+        supply_flat(send_relay, got_relay, relay_sem, 0)
         mirror(send_spill.at[1], got_spill.at[1], spill_sem, 1)
 
     arrived(got_table, table_sem, 0, count - 1)
@@ -449,49 +470,48 @@
         high, low = halves(jnp.concatenate(values, axis=0))
         return dot(select, high) + dot(select, low)
 
-    settle_flat(got_near, 0, near_sem, 0)
-    settle_rise(got_near, 0, near_sem, 1)
-    arrived(got_far.at[0], far_sem, 0, peers)
-    if spill:
-        settle_flat(got_relay, 0, relay_sem, 0)
-        settle_rise(got_relay, 0, relay_sem, 1)
-    pad_a[HALF : HALF + rows, LANES : LANES + cols] = gather(0, slice(None))
-    first = exchange(pad_a, 0, 0, cols)
-    supply(0)
-    supply_near(1, "rise", 3, windows[0])
+    settle_flat(got_near, near_sem, 0)
+    if spill:
+        settle_flat(got_relay, relay_sem, 0)
+    first = []
+    for piece, window in enumerate(windows):
+        left, size = cuts[piece]
+        settle_piece(0, piece)
+        pad_a[HALF : HALF + rows, LANES + left : LANES + left + size] = gather(0, window)
+        first += exchange(pad_a, piece, left, size)
+    for piece in range(AHEAD):
+        supply_rise(send_near, got_near, near_sem, 1, piece)
+        supply_far(1, piece)
     if spill:
         relay(1)
-        supply_relay(1, "flat", 2)
-    for piece, window in enumerate(windows):
-        if piece > 0:
-            supply_near(1, "rise", 3 + piece, window)
+        supply_flat(send_relay, got_relay, relay_sem, 1)
+        for piece in range(AHEAD):
+            supply_rise(send_relay, got_relay, relay_sem, 1, piece)
+    for piece in range(AHEAD, PIECES):
+        supply_rise(send_near, got_near, near_sem, 1, piece)
         if spill:
-            supply_relay(1, "rise", 3 + piece, window)
-        if piece > 0:
-            supply(piece)
+            supply_rise(send_relay, got_relay, relay_sem, 1, piece)
+        supply_far(1, piece)
     for load in loads[4:]:
         load.wait()
     receive(first)
     u_ref[...] = smooth(pad_a)
 
     second = []
-    settle_flat(got_near, 1, near_sem, 2)
-    if spill:
-        settle_flat(got_relay, 1, relay_sem, 2)
+    settle_flat(got_near, near_sem, 1)
+    if spill:
+        settle_flat(got_relay, relay_sem, 1)
     for piece, window in enumerate(windows):
         left, size = cuts[piece]
         inner = slice(LANES + left, LANES + left + size)
-        settle_rise(got_near, 1, near_sem, 3 + piece, window)
-        if spill:
-            settle_rise(got_relay, 1, relay_sem, 3 + piece, window)
-        arrived(got_far.at[1], far_sem, 1 + piece, peers, window)
+        settle_piece(1, piece)
         root = jnp.sqrt(prior_ref[:, window] + gather(1, window))
         root_ref[:, window] = root
         r0_ref[:, window] = pad_a[HALF : HALF + rows, inner] / root
         u = root * u_ref[:, window]
         u_ref[:, window] = u
         pad_b[HALF : HALF + rows, inner] = root * u
-        second += exchange(pad_b, 1 + piece, left, size)
+        second += exchange(pad_b, PIECES + piece, left, size)
     r0, u = r0_ref[...], u_ref[...]
     rr, ru = total(r0 * r0), total(r0 * u)
     own = jnp.where(rr > 0.0, ru / rr, 0.0)
@@ -533,20 +553,17 @@
     finish(second)
     arrived(send_table, table_sem, 0, count - 1, way=0)
     for array in range(2):
-        settle_flat(send_near, array, near_sem, 2 * array, way=0)
-    settle_rise(send_near, 0, near_sem, 1, way=0)
-    arrived(send_far.at[0], far_sem, 0, peers, way=0)
-    for piece, window in enumerate(windows):
-        arrived(send_far.at[1], far_sem, 1 + piece, peers, window, way=0)
-        settle_rise(send_near, 1, near_sem, 3 + piece, window, way=0)
+        settle_flat(send_near, near_sem, array, way=0)
+        for piece in range(PIECES):
+            settle_rise(send_near, near_sem, array, piece, way=0)
+            settle_far(send_far, array, piece, way=0)
         if spill:
-            settle_rise(send_relay, 1, relay_sem, 3 + piece, window, way=0)
+            drain(send_spill.at[array], spill_sem, 0, array)
+            settle_flat(send_relay, relay_sem, array, way=0)
+            for piece in range(PIECES):
+                settle_rise(send_relay, relay_sem, array, piece, way=0)
     if spill:
         drain(send_list, spill_sem, 0, 2)
-        for array in range(2):
-            drain(send_spill.at[array], spill_sem, 0, array)
-            settle_flat(send_relay, array, relay_sem, 2 * array, way=0)
-        settle_rise(send_relay, 0, relay_sem, 1, way=0)
     arrived(parts, part_sem, 0, count - 1, way=0)
 
 
@@ -604,12 +621,12 @@
             scratch(1, LANES),
             scratch(count, 1, LANES),
             semaphores(2, 1),
-            semaphores(2, 3 + PIECES),
-            semaphores(2, 1 + PIECES),
+            semaphores(2, 2 + 2 * PIECES),
+            semaphores(2, 2 * PIECES),
             semaphores(2, 3),
-            semaphores(2, 3 + PIECES),
-            semaphores(1 + PIECES, 8),
-            semaphores(1 + PIECES, 8),
+            semaphores(2, 2 + 2 * PIECES),
+            semaphores(2 * PIECES, 8),
+            semaphores(2 * PIECES, 8),
             semaphores(2, 1),
         ],
         compiler_params=pltpu.CompilerParams(

time: 64 us -> 62 us (0.969)
  Pallas kernels: 62 us -> 60 us
    pallas_call x1, Pallas kernels: 60.4 us -> 58.4 us  [solve(): pl.pallas_call(functools.partial(solve_kernel, ny, nx, slots, direct, roo...]
where the time goes in v1:
time: 62 us; the launch traced here: 61.8 us
  Pallas kernels  60 us (97%)
  between operations  1.29 us (2%)
    pallas_call x1, Pallas kernels, solve(): pl.pallas_call(functools.partial(solve_kernel, ny, nx, slots, direct, roo...  58.4 us
    pallas_call x1, Pallas kernels, close(): pl.pallas_call(close_kernel, out_shape=(shape, shape), in_specs=[vmem] *...  1.59 us

profile of v1, /device:TPU:0, one launch (start us, length us, event | category | flops | bytes accessed | tf_op | source)
XLA Modules:
  0.0 61.8 jit_solution(8355951110700094218)
XLA Ops:
  0.6 58.4 %shard_map.90 = (f32[128,1024]{1,0:T(8,128)S(1)}, f32[128,1024]{1,0:T(8,128)S(1)}, f32[128,1024]{1,0:T(8,128)S(1)}, f32[1,128]{1,0:T(1,128)S(1)}) custom-call(s32[1,128]{1,0:T(1,128)} %bitcast.9, s32[1,128]{1,0:T(1,128)} %bitcast.11, f32[128,8,128]{2,1,0:T(8,128)} %bitcast.5, f32[128,8,128]{2,1,0:T(8,128)} %bitcast.7, f32[128,1024]{1,0:T(8,128)} %prior_hbm.1, ...), custom_call_target="tpu_custom_call" | custom-call | tf_op jit(solution)/shard_map/pallas_call | solution.py:601
  59.0 0.6 slice.3
  60.2 1.6 %conditional.1 = ((f32[128,1024]{1,0:T(8,128)}, f32[128,1024]{1,0:T(8,128)})) conditional(s32[]{:T(128)} %bitcast.4, (f32[128,1024]{1,0:T(8,128)S(1)}, f32[128,1024]{1,0:T(8,128)S(1)}, f32[128,1024]{1,0:T(8,128)S(1)}, f32[1,128]{1,0:T(1,128)S(1)}) %shard_map.90, (s32[1,128]{1,0:T(1,128)}, s32[1,128]{1,0:T(1,128)}, f32[128,8,128]{2,1,0:T(8,128)}, ...), branch_computations={%region_0.0_spmd, %region_1.0_spmd} | conditional | bytes 8 | solution.py:660
  60.2 1.6 %branch_0_fun.1 = (f32[128,1024]{1,0:T(8,128)}, f32[128,1024]{1,0:T(8,128)}) custom-call(f32[128,1024]{1,0:T(8,128)S(1)} %get-tuple-element.24.r0_ref, f32[128,1024]{1,0:T(8,128)S(1)} %get-tuple-element.25.u_ref, f32[128,1024]{1,0:T(8,128)S(1)} %get-tuple-element.26.z_ref, f32[1,128]{1,0:T(1,128)S(1)} %get-tuple-element.27.scalars_ref), custom_call_target="tpu_custom_call" | custom-call | tf_op jit(solution)/shard_map/cond/branch_0_fun/pallas_call | solution.py:641
